TPU v7x, 768 devices: a whole 4x8x12 slice. The times are simulated.
768 devices in a mesh: gx: 12 (over z), gy: 16 (over y, core), band: 4 (over x).
Axes of the slice: x: 4, y: 8, z: 12, core: 2. Of those that a mesh axis runs over, the one named last changes fastest.
Arguments:
- orbitals: float32 [8, 384, 128, 256], P('band', 'gx', 'gy'), may hold values from -600 to 600
- potential: float32 [384, 128, 256], P('gx', 'gy'), may hold values from -0.5 to 0.5
- order: int32 [8], replicated, may hold values from 0 to 7, as said below
Outputs:
- basis: float32 [8, 384, 128, 256], P('band', 'gx', 'gy')
Inputs may be any that keep to these rules, and one draw needn't show every extreme that they name: `order`: each orbital appears once; position p names the orbital orthonormalized p-th.
All inputs are finite; a program needn't handle non-finite values.
Results may differ from a plain program's by a relative error of at most 0.00026.
Values sent between devices are 32-bit elements; how exact they have to be, the bound alone decides.
A program may use at most 32 MiB of HBM per device.

v0:
```python
import jax
import jax.numpy as jnp
from jax import lax
from jax.sharding import PartitionSpec as P

DEGREE = 8


def extended_2(cells, sides, width):
    for axis, dim in sides:
        count = lax.axis_size(axis)
        ends = count - 1
        head = lax.slice_in_dim(cells, 0, width, axis=dim)
        tail = lax.slice_in_dim(cells, cells.shape[dim] - width, cells.shape[dim], axis=dim)
        cells = jnp.concatenate(
            [
                lax.ppermute(tail, axis, [(i, (i + 1) % count) for i in range(ends)]),
                cells,
                lax.ppermute(head, axis, [((i + 1) % count, i) for i in range(ends)]),
            ],
            axis=dim,
        )
    return cells


def apply_operator(extended, potential):
    middle = extended[:, 2:-2, 2:-2, :]
    padded_z = jnp.pad(middle, ((0, 0), (0, 0), (0, 0), (2, 2)))
    nearest = extended[:, 1:-3, 2:-2] + extended[:, 3:-1, 2:-2]
    nearest = nearest + extended[:, 2:-2, 1:-3] + extended[:, 2:-2, 3:-1]
    nearest = nearest + padded_z[..., 1:-3] + padded_z[..., 3:-1]
    distant = extended[:, :-4, 2:-2] + extended[:, 4:, 2:-2]
    distant = distant + extended[:, 2:-2, :-4] + extended[:, 2:-2, 4:]
    distant = distant + padded_z[..., :-4] + padded_z[..., 4:]
    applied = (3.75 + potential) * middle - nearest * (2.0 / 3.0) + distant / 24.0
    return (applied - 4.25 * middle) / 4.25


def mixing_matrix(correlation, order):
    orbital_count = correlation.shape[0]
    positions = jnp.arange(orbital_count, dtype=jnp.int32)
    arrange = (order[:, None] == positions[None, :]).astype(jnp.float32)
    highest = lax.Precision.HIGHEST
    ordered = jnp.dot(
        jnp.dot(arrange, correlation, precision=highest), arrange.T, precision=highest
    )
    lower_factor = jnp.linalg.cholesky(ordered)
    inverse = jax.scipy.linalg.solve_triangular(
        lower_factor, jnp.eye(orbital_count, dtype=jnp.float32), lower=True
    )
    return jnp.dot(jnp.dot(arrange.T, inverse, precision=highest), arrange, precision=highest)


def shallow_step(field, potential):
    extended = extended_2(field, (("gx", 1), ("gy", 2)), 2)
    return apply_operator(extended, potential)


def per_device(orbitals, potential, order):
    group, width_x, width_y, depth_z = orbitals.shape
    previous = orbitals
    current = shallow_step(orbitals, potential)
    for repeat in range(DEGREE - 1):
        following = 2.0 * shallow_step(current, potential) - previous
        previous, current = (current, following)
    gathered = lax.all_gather(current, "band", axis=0, tiled=True)
    flattened = gathered.reshape(gathered.shape[0], -1)
    cell_total = float(width_x * lax.axis_size("gx") * width_y * lax.axis_size("gy") * depth_z)
    band_pos = lax.axis_index("band")
    partial_value = jnp.dot(
        flattened, flattened.T, precision=lax.Precision.HIGHEST, preferred_element_type=jnp.float32
    )
    correlation = lax.psum(partial_value, ("gx", "gy")) / cell_total
    mixing = mixing_matrix(correlation, order)
    own_mixing = lax.dynamic_slice_in_dim(mixing, band_pos * group, group, 0)
    basis = jnp.dot(
        own_mixing, flattened, precision=lax.Precision.HIGHEST, preferred_element_type=jnp.float32
    )
    return basis.reshape(orbitals.shape)


def solution(mesh):
    in_specs = (P("band", "gx", "gy", None), P("gx", "gy", None), P())
    out_specs = P("band", "gx", "gy", None)
    return jax.shard_map(
        per_device, mesh=mesh, in_specs=in_specs, out_specs=out_specs, check_vma=False
    )
```

profile of v0, /device:TPU:2, one launch (start us, length us, event | category | flops | bytes accessed | tf_op | source)
XLA Modules:
  0.0 612.0 jit_solution(4095855693761785779)
XLA Ops:
  6.5 1.3 constant_dynamic-update-slice_fusion.1
  7.8 4.3 collective-permute-start
  12.1 1.3 collective-permute-start.1
  13.7 4.6 collective-permute-done.1
  18.3 1.3 collective-permute-start.2
  19.6 1.3 collective-permute-start.3
  21.1 3.6 collective-permute-done.3
  24.9 0.7 broadcast_multiply_fusion
  25.7 4.4 collective-permute-start.4
  30.1 1.3 collective-permute-start.5
  31.7 5.8 collective-permute-done.5
  37.5 4.6 collective-permute-start.6
  42.1 1.3 collective-permute-start.7
  43.5 2.4 collective-permute-done.7
  46.1 0.8 fusion.94
  46.9 5.1 collective-permute-start.8
  52.1 1.3 collective-permute-start.9
  53.6 4.2 collective-permute-done.9
  57.9 4.6 collective-permute-start.10
  62.5 1.3 collective-permute-start.11
  63.8 2.5 collective-permute-done.11
  66.5 0.8 fusion.81
  67.3 4.6 collective-permute-start.12
  71.9 1.3 collective-permute-start.13
  73.5 4.2 collective-permute-done.13
  77.8 4.6 collective-permute-start.14
  82.4 1.3 collective-permute-start.15
  83.7 2.5 collective-permute-done.15
  86.3 0.7 fusion.68
  87.1 4.0 collective-permute-start.16
  91.1 1.3 collective-permute-start.17
  92.7 4.2 collective-permute-done.17
  96.9 4.6 collective-permute-start.18
  101.6 1.3 collective-permute-start.19
  102.9 2.5 collective-permute-done.19
  105.5 0.7 fusion.55
  106.3 4.6 collective-permute-start.20
  110.9 1.3 collective-permute-start.21
  112.4 4.2 collective-permute-done.21
  116.7 4.6 collective-permute-start.22
  121.3 1.3 collective-permute-start.23
  122.6 2.7 collective-permute-done.23
  125.5 0.7 fusion.42
  126.3 3.7 collective-permute-start.24
  130.0 1.3 collective-permute-start.25
  131.5 4.2 collective-permute-done.25
  135.8 5.5 collective-permute-start.26
  141.3 1.3 collective-permute-start.27
  142.7 2.7 collective-permute-done.27
  145.6 0.7 fusion.29
  146.3 3.6 collective-permute-start.28
  150.0 1.3 collective-permute-start.29
  151.6 4.2 collective-permute-done.29
  155.8 5.5 collective-permute-start.30
  161.4 1.5 collective-permute-start.31
  162.9 2.6 collective-permute-done.31
  165.6 0.7 fusion.16
  166.3 1.1 copy.18
  167.5 45.7 %all-gather.2.cloned.1.call-done = f32[8,32,8,256]{3,2,1,0:T(8,128)} async-done(((f32[2,32,8,256]{3,2,1,0:T(8,128)}), f32[8,32,8,256]{3,2,1,0:T(8,128)}) %all-gather.2.cloned.1.call-update) | async-done | bytes 2097168 | tf_op jit(solution)/shard_map/all_gather | solution.py:66
  213.2 8.3 %fusion.2 = f32[8,8]{1,0:T(8,128)S(1)} fusion(f32[8,32,8,256]{3,2,1,0:T(8,128)} %all-gather.2.cloned.1.call-done), kind=kOutput, calls=%fused_computation.2 | convolution fusion | flops 50331648 | bytes 2097408 | tf_op jit(solution)/shard_map/dot_general | solution.py:70
  221.4 376.0 %psum.7 = f32[8,8]{1,0:T(8,128)S(1)} all-reduce(f32[8,8]{1,0:T(8,128)S(1)} %fusion.2), channel_id=1, replica_groups=mesh['gx'=12,'gy'=16,'band'=4] {'gx','gy'}, use_global_device_ids=true, to_apply=%region_0.1 | all-reduce | flops 64 | bytes 512 | tf_op jit(solution)/shard_map/psum | solution.py:73
  601.2 1.2 copy.25
  602.4 1.9 fusion.151
  604.3 0.8 copy.21
  (66 shorter events, 8.0 us)
Async XLA Ops:
  6.5 14.4 %copy-start.2 = (f32[32,8,256]{2,1,0:T(8,128)S(1)}, f32[32,8,256]{2,1,0:T(8,128)}, u32[]{:S(2)}) copy-start(f32[32,8,256]{2,1,0:T(8,128)} %param.4) | copy-start | bytes 786436
  6.5 206.6 %all-gather.2.cloned.1.call-start = ((), (), s32[]{:S(2)}) async-start(), calls=%async_computation | async-start | bytes 2621440 | tf_op jit(solution)/shard_map/all_gather | solution.py:66
  7.8 5.9 collective-permute-start
  12.1 6.2 %collective-permute-start.1 = (f32[2,2,8,256]{3,1,2,0:T(2,128)S(1)}, f32[2,2,8,256]{3,1,2,0:T(2,128)S(1)}, u32[]{:S(2)}, u32[]{:S(2)}) collective-permute-start(f32[2,2,8,256]{3,1,2,0:T(2,128)S(1)} %get-tuple-element.56), channel_id=1, source_target_pairs={{64,0},{128,64},{192,128},{256,192},{320,256},{384,320},{448,384},... | collective-permute-start | bytes 98312 | tf_op jit(solution)/shard_map/ppermute | solution.py:19
  18.3 2.8 collective-permute-start.2
  19.6 5.1 collective-permute-start.3
  25.6 20.4 %copy-start.1 = (f32[2,32,8,256]{3,2,1,0:T(8,128)S(1)}, f32[2,32,8,256]{3,2,1,0:T(8,128)}, u32[]{:S(2)}) copy-start(f32[2,32,8,256]{3,2,1,0:T(8,128)} %param.3) | copy-start | bytes 1572868
  25.7 6.0 collective-permute-start.4
  30.1 7.4 %collective-permute-start.5 = (f32[2,2,8,256]{3,1,2,0:T(2,128)S(1)}, f32[2,2,8,256]{3,1,2,0:T(2,128)S(1)}, u32[]{:S(2)}, u32[]{:S(2)}) collective-permute-start(f32[2,2,8,256]{3,1,2,0:T(2,128)S(1)} %get-tuple-element.52), channel_id=1, source_target_pairs={{64,0},{128,64},{192,128},{256,192},{320,256},{384,320},{448,384},... | collective-permute-start | bytes 98312 | tf_op jit(solution)/shard_map/ppermute | solution.py:19
  37.5 6.0 collective-permute-start.6
  42.1 3.8 collective-permute-start.7
  46.9 6.7 %collective-permute-start.8 = (f32[2,2,8,256]{3,1,2,0:T(2,128)S(1)}, f32[2,2,8,256]{3,1,2,0:T(2,128)S(1)}, u32[]{:S(2)}, u32[]{:S(2)}) collective-permute-start(f32[2,2,8,256]{3,1,2,0:T(2,128)S(1)} %get-tuple-element.49), channel_id=1, source_target_pairs={{0,64},{64,128},{128,192},{192,256},{256,320},{320,384},{384,448},... | collective-permute-start | bytes 98312 | tf_op jit(solution)/shard_map/ppermute | solution.py:17
  52.1 5.8 collective-permute-start.9
  57.9 5.9 collective-permute-start.10
  62.5 3.8 collective-permute-start.11
  67.3 6.2 %collective-permute-start.12 = (f32[2,2,8,256]{3,1,2,0:T(2,128)S(1)}, f32[2,2,8,256]{3,1,2,0:T(2,128)S(1)}, u32[]{:S(2)}, u32[]{:S(2)}) collective-permute-start(f32[2,2,8,256]{3,1,2,0:T(2,128)S(1)} %get-tuple-element.47), channel_id=1, source_target_pairs={{0,64},{64,128},{128,192},{192,256},{256,320},{320,384},{384,448},... | collective-permute-start | bytes 98312 | tf_op jit(solution)/shard_map/ppermute | solution.py:17
  71.9 5.8 collective-permute-start.13
  77.8 5.9 collective-permute-start.14
  82.4 3.8 collective-permute-start.15
  87.1 5.6 collective-permute-start.16
  91.1 5.8 collective-permute-start.17
  96.9 5.9 collective-permute-start.18
  101.6 3.8 collective-permute-start.19
  106.3 6.2 %collective-permute-start.20 = (f32[2,2,8,256]{3,1,2,0:T(2,128)S(1)}, f32[2,2,8,256]{3,1,2,0:T(2,128)S(1)}, u32[]{:S(2)}, u32[]{:S(2)}) collective-permute-start(f32[2,2,8,256]{3,1,2,0:T(2,128)S(1)} %get-tuple-element.43), channel_id=1, source_target_pairs={{0,64},{64,128},{128,192},{192,256},{256,320},{320,384},{384,448},... | collective-permute-start | bytes 98312 | tf_op jit(solution)/shard_map/ppermute | solution.py:17
  110.9 5.8 collective-permute-start.21
  116.7 5.9 collective-permute-start.22
  121.3 4.0 collective-permute-start.23
  126.3 5.2 collective-permute-start.24
  130.0 5.8 collective-permute-start.25
  135.8 6.8 %collective-permute-start.26 = (f32[2,36,2,256]{3,1,2,0:T(8,128)S(1)}, f32[2,36,2,256]{3,1,2,0:T(8,128)S(1)}, u32[]{:S(2)}, u32[]{:S(2)}) collective-permute-start(f32[2,36,2,256]{3,1,2,0:T(8,128)S(1)} %get-tuple-element.13), channel_id=1, source_target_pairs={{0,4},{4,8},{8,12},{12,16},{16,20},{20,24},{24,28},{28,32},{32,36}... | collective-permute-start | bytes 442376 | tf_op jit(solution)/shard_map/ppermute | solution.py:17
  141.3 4.1 collective-permute-start.27
  146.3 5.2 collective-permute-start.28
  150.0 5.8 collective-permute-start.29
  155.8 7.0 %collective-permute-start.30 = (f32[2,36,2,256]{3,1,2,0:T(8,128)S(1)}, f32[2,36,2,256]{3,1,2,0:T(8,128)S(1)}, u32[]{:S(2)}, u32[]{:S(2)}) collective-permute-start(f32[2,36,2,256]{3,1,2,0:T(8,128)S(1)} %get-tuple-element.9), channel_id=1, source_target_pairs={{0,4},{4,8},{8,12},{12,16},{16,20},{20,24},{24,28},{28,32},{32,36}... | collective-permute-start | bytes 442376 | tf_op jit(solution)/shard_map/ppermute | solution.py:17
  161.4 4.1 collective-permute-start.31
  166.3 431.1 %copy-start.3 = (s32[8]{0:T(128)S(1)}, s32[8]{0:T(128)}, u32[]{:S(2)}) copy-start(s32[8]{0:T(128)} %param.5) | copy-start | bytes 100
  213.2 388.0 %copy-start = (f32[8,32,8,256]{3,2,1,0:T(8,128)S(1)}, f32[8,32,8,256]{3,2,1,0:T(8,128)}, u32[]{:S(2)}) copy-start(f32[8,32,8,256]{3,2,1,0:T(8,128)} %all-gather.2.cloned.1.call-done) | copy-start | bytes 6291460
Sparse Core Ops, SparseCore 0:
  167.6 45.5 all-gather.1
where the time goes:
time: 613 us; the launch traced here: 612 us
  blocking collectives  376 us (61%)
  waiting for transfers between devices  105 us (17%)
  starting transfers between devices  90.6 us (15%)
  between operations  14 us (2%)
  matrix products  11.1 us (2%)
  other arithmetic  10.2 us (2%)
    psum x1, blocking collectives, per_device(): correlation = lax.psum(partial_value, ('gx', 'gy')) / cell_total  376 us
    ppermute x16, starting transfers between devices, extended_2(): lax.ppermute(tail, axis, [(i, (i + 1) % count) for i in range(ends)])  69.7 us
    ppermute x16, waiting for transfers between devices, extended_2(): lax.ppermute(head, axis, [((i + 1) % count, i) for i in range(ends)])  57.2 us
    all_gather x1, waiting for transfers between devices, per_device(): gathered = lax.all_gather(current, 'band', axis=0, tiled=True)  45.7 us
    ppermute x16, starting transfers between devices, extended_2(): lax.ppermute(head, axis, [((i + 1) % count, i) for i in range(ends)])  20.9 us
  transfers between devices with their start and end apart: 33, of which 25 were waited for; matrix products, arithmetic and copies ran while one was open for 0% of the time, Pallas kernels for 0%

commit v1 on v0

v1 whole, which is shorter than its diff:
```python
import functools

import jax
import jax.numpy as jnp
from jax import lax
from jax.experimental import pallas as pl
from jax.experimental.pallas import tpu as pltpu
from jax.sharding import PartitionSpec as P

DEGREE = 8
MESH = pl.DeviceIdType.MESH
F32 = jnp.float32
FAR = 2.0 / (24.0 * 4.25)

NXL, NYL = 32, 8
X0, XROWS, Y0, YROWS = 8, 48, 2, 12


def kernel(sizes, orb_ref, pot_ref, order_ref, out_ref, u, g, pp, v, w, s1, s2, s3, r1, r2, r3,
           hs, hr, as_, ar, bs, br, rs, rr):
    n_gx, n_gy, n_band = sizes
    gx, gy, band = lax.axis_index("gx"), lax.axis_index("gy"), lax.axis_index("band")
    names = (("band", band, n_band), ("gy", gy, n_gy), ("gx", gx, n_gx))

    zero_y = jnp.zeros((2, 2, 2, 2, 32, 128), F32)
    zero_x = jnp.zeros((2, 2, YROWS, 2, 2, 128), F32)

    @pl.when(gy == 0)
    def _():
        u[:, :, 0:2, :, X0:X0 + NXL, :] = zero_y

    @pl.when(gy == n_gy - 1)
    def _():
        u[:, :, 10:12, :, X0:X0 + NXL, :] = zero_y

    @pl.when(gx == 0)
    def _():
        u[:, :, :, :, 6:8, :] = zero_x

    @pl.when(gx == n_gx - 1)
    def _():
        u[:, :, :, :, 40:42, :] = zero_x

    barrier = pltpu.get_barrier_semaphore()
    for name, me, count in names:
        def greet(d, c, name=name, me=me, count=count):
            pl.semaphore_signal(barrier, inc=1, device_id={name: lax.rem(me + d, count)}, device_id_type=MESH)
            return c
        lax.fori_loop(1, count, greet, 0)

    def bring(x, c):
        for zt in range(2):
            for o in range(2):
                v[o, pl.ds(zt * NXL + x, NYL, stride=2 * NXL), :] = orb_ref[o, x, :, zt * 128:zt * 128 + 128]
            w[pl.ds(zt * NXL + x, NYL, stride=2 * NXL), :] = pot_ref[x, :, zt * 128:zt * 128 + 128]
        return c

    lax.fori_loop(0, NXL, bring, 0)

    def place(y, c):
        for zt in range(2):
            for xt in range(4):
                rows_in = pl.ds(y * 64 + zt * NXL + 8 * xt, 8)
                for o in range(2):
                    u[o, 0, Y0 + y, zt, pl.ds(X0 + 8 * xt, 8), :] = v[o, rows_in, :]
                pp[y, zt, pl.ds(8 * xt, 8), :] = (w[rows_in, :] - 0.5) * (2.0 / 4.25)
        return c

    lax.fori_loop(0, NYL, place, 0)
    pl.semaphore_wait(barrier, n_band + n_gy + n_gx - 3)

    sends_ok = (gy > 0, gy < n_gy - 1, gx > 0, gx < n_gx - 1)
    recvs_ok = (gy < n_gy - 1, gy > 0, gx < n_gx - 1, gx > 0)
    ids = ({"gy": gy - 1}, {"gy": gy + 1}, {"gx": gx - 1}, {"gx": gx + 1})
    xs = pl.ds(X0, NXL)
    ys = pl.ds(Y0, NYL)
    spans = (
        ((pl.ds(2, 2), xs), (pl.ds(10, 2), xs)),
        ((pl.ds(8, 2), xs), (pl.ds(0, 2), xs)),
        ((ys, pl.ds(8, 2)), (ys, pl.ds(40, 2))),
        ((ys, pl.ds(38, 2)), (ys, pl.ds(6, 2))),
    )

    def halo(o, p, way):
        (sy, sx), (dy, dx) = spans[way]
        return pltpu.make_async_remote_copy(
            src_ref=u.at[o, p, sy, :, sx, :], dst_ref=u.at[o, p, dy, :, dx, :],
            send_sem=hs.at[o, p, way], recv_sem=hr.at[o, p, way],
            device_id=ids[way], device_id_type=MESH)

    def send(o, p, ways):
        for way in ways:
            @pl.when(sends_ok[way])
            def _(way=way):
                halo(o, p, way).start()

    def arrive(o, p):
        for way in range(4):
            @pl.when(recvs_ok[way])
            def _(way=way):
                halo(o, p, way).wait_recv()

            @pl.when(sends_ok[way])
            def _(way=way):
                halo(o, p, way).wait_send()

    lane = lax.broadcasted_iota(jnp.int32, (8, 128), 1)
    sub = lax.broadcasted_iota(jnp.int32, (8, 128), 0)

    def rows(o, k, lo, hi):
        p = k % 2
        cur, prev = u.at[o, p], u.at[o, 1 - p]

        def body(y, c):
            yy = y + Y0
            for xt in range(4):
                r = X0 + 8 * xt
                mid = [cur[yy, zt, pl.ds(r, 8), :] for zt in range(2)]
                none = jnp.zeros_like(mid[0])
                for zt in range(2):
                    m = mid[zt]
                    after = mid[1] if zt == 0 else none
                    before = mid[0] if zt == 1 else none
                    near = cur[yy, zt, pl.ds(r - 1, 8), :] + cur[yy, zt, pl.ds(r + 1, 8), :]
                    near = near + (cur[yy - 1, zt, pl.ds(r, 8), :] + cur[yy + 1, zt, pl.ds(r, 8), :])
                    near = near + (pltpu.roll(jnp.where(lane < 1, after, m), 127, 1)
                                   + pltpu.roll(jnp.where(lane >= 127, before, m), 1, 1))
                    far = cur[yy, zt, pl.ds(r - 2, 8), :] + cur[yy, zt, pl.ds(r + 2, 8), :]
                    far = far + (cur[yy - 2, zt, pl.ds(r, 8), :] + cur[yy + 2, zt, pl.ds(r, 8), :])
                    far = far + (pltpu.roll(jnp.where(lane < 2, after, m), 126, 1)
                                 + pltpu.roll(jnp.where(lane >= 126, before, m), 2, 1))
                    value = pp[y, zt, pl.ds(8 * xt, 8), :] * m + (far - 16.0 * near) * FAR
                    if k == 0:
                        value = value * 0.5
                    else:
                        value = value - prev[yy, zt, pl.ds(r, 8), :]
                    if k == DEGREE - 1:
                        g[o, band, y, zt, pl.ds(8 * xt, 8), :] = value
                    else:
                        prev[yy, zt, pl.ds(r, 8), :] = value
            return c

        lax.fori_loop(lo, hi, body, 0)

    def quarter(o, d, turn):
        peer = lax.rem(band + d, n_band)
        part = lax.rem(peer + turn, n_band)
        block = g.at[o, band, pl.ds(2 * part, 2)]
        sem = (as_.at[o], ar.at[o]) if turn == 0 else (bs.at[o], br.at[o])
        return pltpu.make_async_remote_copy(
            src_ref=block, dst_ref=block, send_sem=sem[0], recv_sem=sem[1],
            device_id={"band": peer}, device_id_type=MESH)

    for o in range(2):
        send(o, 0, range(4))
    for k in range(DEGREE):
        for o in range(2):
            arrive(o, k % 2)
            last = k == DEGREE - 1
            rows(o, k, 0, 2)
            if not last:
                send(o, 1 - k % 2, (0,))
            rows(o, k, 6, 8)
            if not last:
                send(o, 1 - k % 2, (1,))
            rows(o, k, 2, 6)
            if not last:
                send(o, 1 - k % 2, (2, 3))
            else:
                for d in range(1, n_band):
                    quarter(o, d, 0).start()

    def both(o, first, count, sems):
        block = g.at[o, pl.ds(0, first), pl.ds(0, count)]
        pltpu.make_async_copy(block, block, sems[1].at[o]).wait()
        pltpu.make_async_copy(block, block, sems[0].at[o]).wait()

    for o in range(2):
        both(o, n_band - 1, 2, (as_, ar))

    orbs = 2 * n_band
    pairs = [(i, j) for i in range(orbs) for j in range(i + 1)]

    def correlate(t, sums):
        y, zt = 2 * band + t // 2, t % 2
        sums = list(sums)
        for xt in range(4):
            f = [g[i % 2, i // 2, y, zt, pl.ds(8 * xt, 8), :] for i in range(orbs)]
            sums = [a + f[i] * f[j] for a, (i, j) in zip(sums, pairs)]
        return tuple(sums)

    sums = lax.fori_loop(0, 4, correlate, tuple(jnp.zeros((8, 128), F32) for _ in pairs))
    flat = {}
    for a, (i, j) in zip(sums, pairs):
        flat[i, j] = flat[j, i] = jnp.sum(a, axis=0, keepdims=True)
    corr = jnp.zeros((8, 128), F32)
    for j in range(orbs):
        column = jnp.sum(jnp.concatenate([flat[i, j] for i in range(orbs)], axis=0), axis=1, keepdims=True)
        corr = jnp.where(lane == j, column, corr)

    for index, ((name, me, count), src, dst) in enumerate(zip(names, (s1, s2, s3), (r1, r2, r3))):
        src[...] = corr

        def give(d, c, name=name, me=me, count=count, src=src, dst=dst, index=index):
            pltpu.make_async_remote_copy(
                src_ref=src, dst_ref=dst.at[d - 1], send_sem=rs.at[index], recv_sem=rr.at[index],
                device_id={name: lax.rem(me + d, count)}, device_id_type=MESH).start()
            return c

        lax.fori_loop(1, count, give, 0)
        if index == 0:
            for turn in range(1, n_band):
                for o in range(2):
                    for d in range(1, n_band):
                        quarter(o, d, turn).start()
        pltpu.make_async_copy(dst, dst, rr.at[index]).wait()
        for d in range(count - 1):
            corr = corr + dst[d]
    cells = float(n_gx * NXL * n_gy * NYL * 256)
    state = jnp.where(lane < 8, corr * (1.0 / cells), jnp.where(lane == sub + 8, 1.0, 0.0))
    waiting = jnp.ones((8, 128), F32)
    pivots = jnp.ones((8, 128), F32)
    for position in range(orbs):
        j = order_ref[position]
        row = jnp.sum(jnp.where(sub == j, state, 0.0), axis=0, keepdims=True)
        column = jnp.sum(jnp.where(lane == j, state, 0.0), axis=1, keepdims=True)
        pivot = jnp.sum(jnp.where(lane[0:1] == j, row, 0.0), axis=1, keepdims=True)
        waiting = jnp.where(sub == j, 0.0, waiting)
        state = state - (waiting * (column / pivot)) * row
        pivots = jnp.where(sub == j, pivot, pivots)
    mixing = state / jnp.sqrt(pivots)

    weights = []
    for o in range(2):
        own = jnp.sum(jnp.where(sub == 2 * band + o, mixing, 0.0), axis=0, keepdims=True)
        weights.append([jnp.broadcast_to(jnp.sum(jnp.where(lane[0:1] == 8 + j, own, 0.0), axis=1, keepdims=True), (8, 128))
                        for j in range(orbs)])

    for o in range(2):
        both(o, n_band - 1, 6, (bs, br))
    for index, dst in enumerate((r1, r2, r3)):
        pltpu.make_async_copy(dst, dst, rs.at[index]).wait()

    def combine(y, c):
        for zt in range(2):
            for xt in range(4):
                f = [g[i % 2, i // 2, y, zt, pl.ds(8 * xt, 8), :] for i in range(orbs)]
                for o in range(2):
                    total = weights[o][0] * f[0]
                    for i in range(1, orbs):
                        total = total + weights[o][i] * f[i]
                    v[o, pl.ds(y * 64 + zt * 32 + 8 * xt, 8), :] = total
        return c

    lax.fori_loop(0, NYL, combine, 0)

    def hand_back(x, c):
        for o in range(2):
            for zt in range(2):
                out_ref[o, x, :, zt * 128:zt * 128 + 128] = v[o, pl.ds(zt * 32 + x, 8, stride=64), :]
        return c

    lax.fori_loop(0, NXL, hand_back, 0)


def solution(mesh):
    sizes = tuple(mesh.shape[name] for name in ("gx", "gy", "band"))
    n_gx, n_gy, n_band = sizes

    def per_device(orbitals, potential, order):
        sem = pltpu.SemaphoreType.DMA
        return pl.pallas_call(
            functools.partial(kernel, sizes),
            out_shape=jax.ShapeDtypeStruct(orbitals.shape, F32),
            in_specs=[pl.BlockSpec(memory_space=pltpu.VMEM), pl.BlockSpec(memory_space=pltpu.VMEM),
                      pl.BlockSpec(memory_space=pltpu.SMEM)],
            out_specs=pl.BlockSpec(memory_space=pltpu.VMEM),
            scratch_shapes=[
                pltpu.VMEM((2, 2, YROWS, 2, XROWS, 128), F32),
                pltpu.VMEM((2, n_band, NYL, 2, NXL, 128), F32),
                pltpu.VMEM((NYL, 2, NXL, 128), F32),
                pltpu.VMEM((2, NYL * 2 * NXL, 128), F32),
                pltpu.VMEM((NYL * 2 * NXL, 128), F32),
                pltpu.VMEM((8, 128), F32), pltpu.VMEM((8, 128), F32), pltpu.VMEM((8, 128), F32),
                pltpu.VMEM((n_band - 1, 8, 128), F32), pltpu.VMEM((n_gy - 1, 8, 128), F32),
                pltpu.VMEM((n_gx - 1, 8, 128), F32),
                sem((2, 2, 4)), sem((2, 2, 4)),
                sem((2,)), sem((2,)), sem((2,)), sem((2,)), sem((3,)), sem((3,)),
            ],
            compiler_params=pltpu.CompilerParams(
                collective_id=0, has_side_effects=True, vmem_limit_bytes=32 * 1024 * 1024),
        )(orbitals, potential, order)

    return jax.shard_map(
        per_device, mesh=mesh,
        in_specs=(P("band", "gx", "gy", None), P("gx", "gy", None), P()),
        out_specs=P("band", "gx", "gy", None), check_vma=False,
    )
```

time: 613 us -> 82.8 us (0.14)
  the two profiles are of different devices: /device:TPU:2 before, /device:TPU:24 now
where the time goes in v1:
time: 82.8 us; the launch traced here: 82.6 us
  Pallas kernels  79.1 us (96%)
  local copies, waits for them, and re-layouts  3.44 us (4%)
    pallas_call x1, Pallas kernels, per_device(): pl.pallas_call(functools.partial(kernel, sizes), out_shape=jax.ShapeDtype...  79.1 us
    unnamed x7, local copies, waits for them, and re-layouts  3.44 us

profile of v1, /device:TPU:24, one launch (start us, length us, event | category | flops | bytes accessed | tf_op | source)
XLA Modules:
  0.0 82.6 jit_solution(3066858484825231800)
XLA Ops:
  0.0 0.0 copy-start
  0.0 1.0 %copy-done = f32[2,32,8,256]{3,2,1,0:T(8,128)S(1)} copy-done((f32[2,32,8,256]{3,2,1,0:T(8,128)S(1)}, f32[2,32,8,256]{3,2,1,0:T(8,128)}, u32[]{:S(2)}) %copy-start) | copy-done | bytes 524312
  1.0 0.0 copy-start.1
  1.0 0.9 %copy-done.1 = f32[32,8,256]{2,1,0:T(8,128)S(1)} copy-done((f32[32,8,256]{2,1,0:T(8,128)S(1)}, f32[32,8,256]{2,1,0:T(8,128)}, u32[]{:S(2)}) %copy-start.1) | copy-done | bytes 262168
  2.0 0.0 copy-start.2
  2.0 0.7 copy-done.2
  2.6 79.1 %shard_map.37 = f32[2,32,8,256]{3,2,1,0:T(8,128)S(1)} custom-call(f32[2,32,8,256]{3,2,1,0:T(8,128)S(1)} %copy-done, f32[32,8,256]{2,1,0:T(8,128)S(1)} %copy-done.1, s32[8]{0:T(128)S(1)} %copy-done.2), custom_call_target="tpu_custom_call" | custom-call | tf_op jit(solution)/shard_map/pallas_call | solution.py:272
  81.8 0.8 copy.5
Async XLA Ops:
  0.0 1.0 %copy-start = (f32[2,32,8,256]{3,2,1,0:T(8,128)S(1)}, f32[2,32,8,256]{3,2,1,0:T(8,128)}, u32[]{:S(2)}) copy-start(f32[2,32,8,256]{3,2,1,0:T(8,128)} %orb_ref.1) | copy-start | bytes 1572868
  1.0 0.9 %copy-start.1 = (f32[32,8,256]{2,1,0:T(8,128)S(1)}, f32[32,8,256]{2,1,0:T(8,128)}, u32[]{:S(2)}) copy-start(f32[32,8,256]{2,1,0:T(8,128)} %pot_ref.1) | copy-start | bytes 786436
  2.0 0.7 copy-start.2

commit v2 on v1

--- a/solution.py
+++ b/solution.py
@@ -13,33 +13,36 @@
 FAR = 2.0 / (24.0 * 4.25)
 
 NXL, NYL = 32, 8
-X0, XROWS, Y0, YROWS = 8, 48, 2, 12
-
-
-def kernel(sizes, orb_ref, pot_ref, order_ref, out_ref, u, g, pp, v, w, s1, s2, s3, r1, r2, r3,
-           hs, hr, as_, ar, bs, br, rs, rr):
+X0, XROWS, Y0, YROWS = 8, 48, 4, 16
+
+
+def kernel(sizes, orb_ref, pot_ref, order_ref, out_ref, a0, a1, b0, b1, g, pp, v, w, s1, s2, s3, r1, r2, r3,
+           hs, hr, ps, pr, as_, ar, bs, br, rs, rr):
     n_gx, n_gy, n_band = sizes
     gx, gy, band = lax.axis_index("gx"), lax.axis_index("gy"), lax.axis_index("band")
     names = (("band", band, n_band), ("gy", gy, n_gy), ("gx", gx, n_gx))
 
-    zero_y = jnp.zeros((2, 2, 2, 2, 32, 128), F32)
-    zero_x = jnp.zeros((2, 2, YROWS, 2, 2, 128), F32)
-
-    @pl.when(gy == 0)
-    def _():
-        u[:, :, 0:2, :, X0:X0 + NXL, :] = zero_y
-
-    @pl.when(gy == n_gy - 1)
-    def _():
-        u[:, :, 10:12, :, X0:X0 + NXL, :] = zero_y
-
-    @pl.when(gx == 0)
-    def _():
-        u[:, :, :, :, 6:8, :] = zero_x
-
-    @pl.when(gx == n_gx - 1)
-    def _():
-        u[:, :, :, :, 40:42, :] = zero_x
+    def clear(ref, *index):
+        view = ref.at[index]
+        view[...] = jnp.zeros(view.shape, F32)
+
+    for ref in (a0, a1, b0, b1):
+        for o in range(2):
+            @pl.when(gy == 0)
+            def _(ref=ref, o=o):
+                clear(ref, o, slice(0, 4))
+
+            @pl.when(gy == n_gy - 1)
+            def _(ref=ref, o=o):
+                clear(ref, o, slice(12, 16))
+
+            @pl.when(gx == 0)
+            def _(ref=ref, o=o):
+                clear(ref, o, slice(2, 14), slice(None), slice(0, 8))
+
+            @pl.when(gx == n_gx - 1)
+            def _(ref=ref, o=o):
+                clear(ref, o, slice(2, 14), slice(None), slice(40, 48))
 
     barrier = pltpu.get_barrier_semaphore()
     for name, me, count in names:
@@ -47,6 +50,15 @@
             pl.semaphore_signal(barrier, inc=1, device_id={name: lax.rem(me + d, count)}, device_id_type=MESH)
             return c
         lax.fori_loop(1, count, greet, 0)
+    corners = [(gx > 0, gy > 0, -1, -1), (gx > 0, gy < n_gy - 1, -1, 1),
+               (gx < n_gx - 1, gy > 0, 1, -1), (gx < n_gx - 1, gy < n_gy - 1, 1, 1)]
+    diagonal = [jnp.logical_and(cx, cy) for cx, cy, _, _ in corners]
+    met = n_band + n_gy + n_gx - 3
+    for ok, (_, _, dx, dy) in zip(diagonal, corners):
+        @pl.when(ok)
+        def _(dx=dx, dy=dy):
+            pl.semaphore_signal(barrier, inc=1, device_id={"gx": gx + dx, "gy": gy + dy}, device_id_type=MESH)
+        met = met + ok.astype(jnp.int32)
 
     def bring(x, c):
         for zt in range(2):
@@ -62,85 +74,139 @@
             for xt in range(4):
                 rows_in = pl.ds(y * 64 + zt * NXL + 8 * xt, 8)
                 for o in range(2):
-                    u[o, 0, Y0 + y, zt, pl.ds(X0 + 8 * xt, 8), :] = v[o, rows_in, :]
-                pp[y, zt, pl.ds(8 * xt, 8), :] = (w[rows_in, :] - 0.5) * (2.0 / 4.25)
+                    a0[o, Y0 + y, zt, pl.ds(X0 + 8 * xt, 8), :] = v[o, rows_in, :]
+                pp[y + 2, zt, pl.ds(X0 + 8 * xt, 8), :] = (w[rows_in, :] - 0.5) * (2.0 / 4.25)
         return c
 
     lax.fori_loop(0, NYL, place, 0)
-    pl.semaphore_wait(barrier, n_band + n_gy + n_gx - 3)
-
-    sends_ok = (gy > 0, gy < n_gy - 1, gx > 0, gx < n_gx - 1)
-    recvs_ok = (gy < n_gy - 1, gy > 0, gx < n_gx - 1, gx > 0)
-    ids = ({"gy": gy - 1}, {"gy": gy + 1}, {"gx": gx - 1}, {"gx": gx + 1})
-    xs = pl.ds(X0, NXL)
-    ys = pl.ds(Y0, NYL)
-    spans = (
+    pl.semaphore_wait(barrier, met)
+
+    low_x, high_x, low_y, high_y = gx > 0, gx < n_gx - 1, gy > 0, gy < n_gy - 1
+    sends_ok = [low_y, high_y, low_x, high_x] + diagonal
+    recvs_ok = [high_y, low_y, high_x, low_x] + diagonal[::-1]
+    ids = [{"gy": gy - 1}, {"gy": gy + 1}, {"gx": gx - 1}, {"gx": gx + 1}] + [
+        {"gx": gx + dx, "gy": gy + dy} for _, _, dx, dy in corners]
+    xs, ys = pl.ds(X0, NXL), pl.ds(Y0, NYL)
+    spans = [
+        ((pl.ds(4, 4), xs), (pl.ds(12, 4), xs)),
+        ((pl.ds(8, 4), xs), (pl.ds(0, 4), xs)),
+        ((ys, pl.ds(8, 4)), (ys, pl.ds(40, 4))),
+        ((ys, pl.ds(36, 4)), (ys, pl.ds(4, 4))),
+        ((pl.ds(4, 2), pl.ds(8, 2)), (pl.ds(12, 2), pl.ds(40, 2))),
+        ((pl.ds(10, 2), pl.ds(8, 2)), (pl.ds(2, 2), pl.ds(40, 2))),
+        ((pl.ds(4, 2), pl.ds(38, 2)), (pl.ds(12, 2), pl.ds(6, 2))),
+        ((pl.ds(10, 2), pl.ds(38, 2)), (pl.ds(2, 2), pl.ds(6, 2))),
+    ]
+    yp = pl.ds(2, NYL)
+    pot_spans = [
         ((pl.ds(2, 2), xs), (pl.ds(10, 2), xs)),
         ((pl.ds(8, 2), xs), (pl.ds(0, 2), xs)),
-        ((ys, pl.ds(8, 2)), (ys, pl.ds(40, 2))),
-        ((ys, pl.ds(38, 2)), (ys, pl.ds(6, 2))),
-    )
+        ((yp, pl.ds(8, 2)), (yp, pl.ds(40, 2))),
+        ((yp, pl.ds(38, 2)), (yp, pl.ds(6, 2))),
+    ]
+
+    even, odd = (a0, a1), (b0, b1)
 
     def halo(o, p, way):
         (sy, sx), (dy, dx) = spans[way]
         return pltpu.make_async_remote_copy(
-            src_ref=u.at[o, p, sy, :, sx, :], dst_ref=u.at[o, p, dy, :, dx, :],
+            src_ref=even[p].at[o, sy, :, sx, :], dst_ref=even[p].at[o, dy, :, dx, :],
             send_sem=hs.at[o, p, way], recv_sem=hr.at[o, p, way],
             device_id=ids[way], device_id_type=MESH)
 
-    def send(o, p, ways):
+    def pot_halo(way):
+        (sy, sx), (dy, dx) = pot_spans[way]
+        return pltpu.make_async_remote_copy(
+            src_ref=pp.at[sy, :, sx, :], dst_ref=pp.at[dy, :, dx, :],
+            send_sem=ps.at[way], recv_sem=pr.at[way], device_id=ids[way], device_id_type=MESH)
+
+    def send(ways, copy):
         for way in ways:
             @pl.when(sends_ok[way])
             def _(way=way):
-                halo(o, p, way).start()
-
-    def arrive(o, p):
-        for way in range(4):
+                copy(way).start()
+
+    def arrive(ways, copy):
+        for way in ways:
             @pl.when(recvs_ok[way])
             def _(way=way):
-                halo(o, p, way).wait_recv()
+                copy(way).wait_recv()
 
             @pl.when(sends_ok[way])
             def _(way=way):
-                halo(o, p, way).wait_send()
+                copy(way).wait_send()
 
     lane = lax.broadcasted_iota(jnp.int32, (8, 128), 1)
     sub = lax.broadcasted_iota(jnp.int32, (8, 128), 0)
 
-    def rows(o, k, lo, hi):
-        p = k % 2
-        cur, prev = u.at[o, p], u.at[o, 1 - p]
-
-        def body(y, c):
-            yy = y + Y0
-            for xt in range(4):
-                r = X0 + 8 * xt
-                mid = [cur[yy, zt, pl.ds(r, 8), :] for zt in range(2)]
-                none = jnp.zeros_like(mid[0])
-                for zt in range(2):
-                    m = mid[zt]
-                    after = mid[1] if zt == 0 else none
-                    before = mid[0] if zt == 1 else none
-                    near = cur[yy, zt, pl.ds(r - 1, 8), :] + cur[yy, zt, pl.ds(r + 1, 8), :]
-                    near = near + (cur[yy - 1, zt, pl.ds(r, 8), :] + cur[yy + 1, zt, pl.ds(r, 8), :])
-                    near = near + (pltpu.roll(jnp.where(lane < 1, after, m), 127, 1)
-                                   + pltpu.roll(jnp.where(lane >= 127, before, m), 1, 1))
-                    far = cur[yy, zt, pl.ds(r - 2, 8), :] + cur[yy, zt, pl.ds(r + 2, 8), :]
-                    far = far + (cur[yy - 2, zt, pl.ds(r, 8), :] + cur[yy + 2, zt, pl.ds(r, 8), :])
-                    far = far + (pltpu.roll(jnp.where(lane < 2, after, m), 126, 1)
-                                 + pltpu.roll(jnp.where(lane >= 126, before, m), 2, 1))
-                    value = pp[y, zt, pl.ds(8 * xt, 8), :] * m + (far - 16.0 * near) * FAR
-                    if k == 0:
-                        value = value * 0.5
-                    else:
-                        value = value - prev[yy, zt, pl.ds(r, 8), :]
-                    if k == DEGREE - 1:
-                        g[o, band, y, zt, pl.ds(8 * xt, 8), :] = value
-                    else:
-                        prev[yy, zt, pl.ds(r, 8), :] = value
-            return c
-
-        lax.fori_loop(lo, hi, body, 0)
+    def cells(cur, prev, yy, r):
+        mid = [cur[yy, zt, pl.ds(r, 8), :] for zt in range(2)]
+        none = jnp.zeros_like(mid[0])
+        values = []
+        for zt in range(2):
+            m = mid[zt]
+            after = mid[1] if zt == 0 else none
+            before = mid[0] if zt == 1 else none
+            near = cur[yy, zt, pl.ds(r - 1, 8), :] + cur[yy, zt, pl.ds(r + 1, 8), :]
+            near = near + (cur[yy - 1, zt, pl.ds(r, 8), :] + cur[yy + 1, zt, pl.ds(r, 8), :])
+            near = near + (pltpu.roll(jnp.where(lane < 1, after, m), 127, 1)
+                           + pltpu.roll(jnp.where(lane >= 127, before, m), 1, 1))
+            far = cur[yy, zt, pl.ds(r - 2, 8), :] + cur[yy, zt, pl.ds(r + 2, 8), :]
+            far = far + (cur[yy - 2, zt, pl.ds(r, 8), :] + cur[yy + 2, zt, pl.ds(r, 8), :])
+            far = far + (pltpu.roll(jnp.where(lane < 2, after, m), 126, 1)
+                         + pltpu.roll(jnp.where(lane >= 126, before, m), 2, 1))
+            value = pp[yy - 2, zt, pl.ds(r, 8), :] * m + (far - 16.0 * near) * FAR
+            values.append(value * 0.5 if prev is None else value - prev[yy, zt, pl.ds(r, 8), :])
+        return values
+
+    ALIGNED = (8, 16, 24, 32)
+    SHIFTED = (6, 14, 22, 30, 38)
+
+    def odd_step(o, j):
+        p = j % 2
+        cur, prev, new = even[p].at[o], None if j == 0 else odd[1 - p].at[o], odd[p].at[o]
+
+        def put(y, offsets):
+            for r in offsets:
+                for zt, value in enumerate(cells(cur, prev, y, r)):
+                    new[y, zt, pl.ds(r, 8), :] = value
+
+        for y in range(4, 12):
+            put(y, SHIFTED)
+        for ok, y in ((low_y, 2), (high_y, 12)):
+            @pl.when(ok)
+            def _(y=y):
+                put(y, ALIGNED)
+                put(y + 1, ALIGNED)
+
+        @pl.when(gx == 0)
+        def _():
+            new[4:12, :, 6:8, :] = jnp.zeros((8, 2, 2, 128), F32)
+
+        @pl.when(gx == n_gx - 1)
+        def _():
+            new[4:12, :, 40:42, :] = jnp.zeros((8, 2, 2, 128), F32)
+
+    def even_step(o, j):
+        p = j % 2
+        cur, prev, new = odd[p].at[o], even[p].at[o], even[1 - p].at[o]
+        last = j == DEGREE // 2 - 1
+
+        def half(i):
+            for y in range(4 + 4 * i, 8 + 4 * i):
+                for r in ALIGNED:
+                    for zt, value in enumerate(cells(cur, prev, y, r)):
+                        if last:
+                            g[o, band, y - 4, zt, pl.ds(r - X0, 8), :] = value
+                        else:
+                            new[y, zt, pl.ds(r, 8), :] = value
+
+        half(0)
+        if not last:
+            send((0,), functools.partial(halo, o, 1 - p))
+        half(1)
+        if not last:
+            send((1, 2, 3, 4, 5, 6, 7), functools.partial(halo, o, 1 - p))
 
     def quarter(o, d, turn):
         peer = lax.rem(band + d, n_band)
@@ -152,23 +218,25 @@
             device_id={"band": peer}, device_id_type=MESH)
 
     for o in range(2):
-        send(o, 0, range(4))
-    for k in range(DEGREE):
-        for o in range(2):
-            arrive(o, k % 2)
-            last = k == DEGREE - 1
-            rows(o, k, 0, 2)
-            if not last:
-                send(o, 1 - k % 2, (0,))
-            rows(o, k, 6, 8)
-            if not last:
-                send(o, 1 - k % 2, (1,))
-            rows(o, k, 2, 6)
-            if not last:
-                send(o, 1 - k % 2, (2, 3))
-            else:
+        send(range(8), functools.partial(halo, o, 0))
+        if o == 0:
+            send(range(4), pot_halo)
+
+    for j in range(DEGREE // 2):
+        def block(o, c, j=j):
+            arrive(range(8), functools.partial(halo, o, j % 2))
+            if j == 0:
+                @pl.when(o == 0)
+                def _():
+                    arrive(range(4), pot_halo)
+            odd_step(o, j)
+            even_step(o, j)
+            if j == DEGREE // 2 - 1:
                 for d in range(1, n_band):
                     quarter(o, d, 0).start()
+            return c
+
+        lax.fori_loop(0, 2, block, 0)
 
     def both(o, first, count, sems):
         block = g.at[o, pl.ds(0, first), pl.ds(0, count)]
@@ -216,8 +284,8 @@
         pltpu.make_async_copy(dst, dst, rr.at[index]).wait()
         for d in range(count - 1):
             corr = corr + dst[d]
-    cells = float(n_gx * NXL * n_gy * NYL * 256)
-    state = jnp.where(lane < 8, corr * (1.0 / cells), jnp.where(lane == sub + 8, 1.0, 0.0))
+    total_cells = float(n_gx * NXL * n_gy * NYL * 256)
+    state = jnp.where(lane < 8, corr * (1.0 / total_cells), jnp.where(lane == sub + 8, 1.0, 0.0))
     waiting = jnp.ones((8, 128), F32)
     pivots = jnp.ones((8, 128), F32)
     for position in range(orbs):
@@ -276,15 +344,15 @@
                       pl.BlockSpec(memory_space=pltpu.SMEM)],
             out_specs=pl.BlockSpec(memory_space=pltpu.VMEM),
             scratch_shapes=[
-                pltpu.VMEM((2, 2, YROWS, 2, XROWS, 128), F32),
+                *[pltpu.VMEM((2, YROWS, 2, XROWS, 128), F32)] * 4,
                 pltpu.VMEM((2, n_band, NYL, 2, NXL, 128), F32),
-                pltpu.VMEM((NYL, 2, NXL, 128), F32),
+                pltpu.VMEM((NYL + 4, 2, XROWS, 128), F32),
                 pltpu.VMEM((2, NYL * 2 * NXL, 128), F32),
                 pltpu.VMEM((NYL * 2 * NXL, 128), F32),
                 pltpu.VMEM((8, 128), F32), pltpu.VMEM((8, 128), F32), pltpu.VMEM((8, 128), F32),
                 pltpu.VMEM((n_band - 1, 8, 128), F32), pltpu.VMEM((n_gy - 1, 8, 128), F32),
                 pltpu.VMEM((n_gx - 1, 8, 128), F32),
-                sem((2, 2, 4)), sem((2, 2, 4)),
+                sem((2, 2, 8)), sem((2, 2, 8)), sem((4,)), sem((4,)),
                 sem((2,)), sem((2,)), sem((2,)), sem((2,)), sem((3,)), sem((3,)),
             ],
             compiler_params=pltpu.CompilerParams(

time: 82.8 us -> 72.2 us (0.87)
  Pallas kernels: 79.1 us -> 68.6 us
    pallas_call x1, Pallas kernels: 79.1 us -> 68.6 us  [per_device(): pl.pallas_call(functools.partial(kernel, sizes), out_shape=jax.ShapeDtype...]
where the time goes in v2:
time: 72.2 us; the launch traced here: 72 us
  Pallas kernels  68.6 us (95%)
  local copies, waits for them, and re-layouts  3.44 us (5%)
    pallas_call x1, Pallas kernels, per_device(): pl.pallas_call(functools.partial(kernel, sizes), out_shape=jax.ShapeDtype...  68.6 us
    unnamed x7, local copies, waits for them, and re-layouts  3.44 us

profile of v2, /device:TPU:24, one launch (start us, length us, event | category | flops | bytes accessed | tf_op | source)
XLA Modules:
  0.0 72.0 jit_solution(5393090446449364831)
XLA Ops:
  0.0 0.0 copy-start
  0.0 1.0 %copy-done = f32[2,32,8,256]{3,2,1,0:T(8,128)S(1)} copy-done((f32[2,32,8,256]{3,2,1,0:T(8,128)S(1)}, f32[2,32,8,256]{3,2,1,0:T(8,128)}, u32[]{:S(2)}) %copy-start) | copy-done | bytes 524312
  1.0 0.0 copy-start.1
  1.0 0.9 %copy-done.1 = f32[32,8,256]{2,1,0:T(8,128)S(1)} copy-done((f32[32,8,256]{2,1,0:T(8,128)S(1)}, f32[32,8,256]{2,1,0:T(8,128)}, u32[]{:S(2)}) %copy-start.1) | copy-done | bytes 262168
  2.0 0.0 copy-start.2
  2.0 0.7 copy-done.2
  2.6 68.6 %shard_map.37 = f32[2,32,8,256]{3,2,1,0:T(8,128)S(1)} custom-call(f32[2,32,8,256]{3,2,1,0:T(8,128)S(1)} %copy-done, f32[32,8,256]{2,1,0:T(8,128)S(1)} %copy-done.1, s32[8]{0:T(128)S(1)} %copy-done.2), custom_call_target="tpu_custom_call" | custom-call | tf_op jit(solution)/shard_map/pallas_call | solution.py:340
  71.2 0.8 %copy.5 = f32[2,32,8,256]{3,2,1,0:T(8,128)} copy(f32[2,32,8,256]{3,2,1,0:T(8,128)S(1)} %shard_map.37) | data formatting | bytes 1048576
Async XLA Ops:
  0.0 1.0 %copy-start = (f32[2,32,8,256]{3,2,1,0:T(8,128)S(1)}, f32[2,32,8,256]{3,2,1,0:T(8,128)}, u32[]{:S(2)}) copy-start(f32[2,32,8,256]{3,2,1,0:T(8,128)} %orb_ref.1) | copy-start | bytes 1572868
  1.0 0.9 %copy-start.1 = (f32[32,8,256]{2,1,0:T(8,128)S(1)}, f32[32,8,256]{2,1,0:T(8,128)}, u32[]{:S(2)}) copy-start(f32[32,8,256]{2,1,0:T(8,128)} %pot_ref.1) | copy-start | bytes 786436
  2.0 0.7 copy-start.2

commit v3 on v2

--- a/solution.py
+++ b/solution.py
@@ -17,7 +17,7 @@
 
 
 def kernel(sizes, orb_ref, pot_ref, order_ref, out_ref, a0, a1, b0, b1, g, pp, v, w, s1, s2, s3, r1, r2, r3,
-           hs, hr, ps, pr, as_, ar, bs, br, rs, rr):
+           hs, hr, ps, pr, as_, ar, bs, br, fr, rs, rr):
     n_gx, n_gy, n_band = sizes
     gx, gy, band = lax.axis_index("gx"), lax.axis_index("gy"), lax.axis_index("band")
     names = (("band", band, n_band), ("gy", gy, n_gy), ("gx", gx, n_gx))
@@ -208,14 +208,44 @@
         if not last:
             send((1, 2, 3, 4, 5, 6, 7), functools.partial(halo, o, 1 - p))
 
-    def quarter(o, d, turn):
-        peer = lax.rem(band + d, n_band)
-        part = lax.rem(peer + turn, n_band)
-        block = g.at[o, band, pl.ds(2 * part, 2)]
-        sem = (as_.at[o], ar.at[o]) if turn == 0 else (bs.at[o], br.at[o])
+    def piece(o, source, part, peer, sends, recvs):
+        block = g.at[o, source, pl.ds(2 * part, 2)]
         return pltpu.make_async_remote_copy(
-            src_ref=block, dst_ref=block, send_sem=sem[0], recv_sem=sem[1],
+            src_ref=block, dst_ref=block, send_sem=sends, recv_sem=recvs,
             device_id={"band": peer}, device_id_type=MESH)
+
+    def around(step):
+        return lax.rem(band + step + n_band, n_band)
+
+    right, left, across = around(1), around(-1), around(2)
+
+    def quarter(o, peer):
+        return piece(o, band, peer, peer, as_.at[o], ar.at[o])
+
+    def own_ahead():
+        for part in (left, band):
+            piece(0, band, part, right, bs.at[0], fr.at[0]).start()
+        for part in (band, right):
+            piece(1, band, part, left, bs.at[1], fr.at[1]).start()
+
+    def own_rest():
+        piece(0, band, across, right, bs.at[0], br.at[0]).start()
+        piece(1, band, across, left, bs.at[1], br.at[1]).start()
+        for part in (band, right, across):
+            piece(0, band, part, left, bs.at[0], br.at[0]).start()
+        for part in (band, left, across):
+            piece(1, band, part, right, bs.at[1], br.at[1]).start()
+
+    def pass_on(parts_right, parts_left):
+        for part in parts_right:
+            piece(0, left, part, right, bs.at[0], br.at[0]).start()
+        for part in parts_left:
+            piece(1, right, part, left, bs.at[1], br.at[1]).start()
+
+    def passed_in():
+        for o in range(2):
+            block = g.at[o, 0, pl.ds(0, 4)]
+            pltpu.make_async_copy(block, block, fr.at[o]).wait()
 
     for o in range(2):
         send(range(8), functools.partial(halo, o, 0))
@@ -232,8 +262,8 @@
             odd_step(o, j)
             even_step(o, j)
             if j == DEGREE // 2 - 1:
-                for d in range(1, n_band):
-                    quarter(o, d, 0).start()
+                for peer in (right, left, across):
+                    quarter(o, peer).start()
             return c
 
         lax.fori_loop(0, 2, block, 0)
@@ -277,10 +307,12 @@
 
         lax.fori_loop(1, count, give, 0)
         if index == 0:
-            for turn in range(1, n_band):
-                for o in range(2):
-                    for d in range(1, n_band):
-                        quarter(o, d, turn).start()
+            own_ahead()
+            pass_on((band,), (band,))
+            own_rest()
+        if index == 1:
+            passed_in()
+            pass_on((left, across), (right, across))
         pltpu.make_async_copy(dst, dst, rr.at[index]).wait()
         for d in range(count - 1):
             corr = corr + dst[d]
@@ -305,7 +337,10 @@
                         for j in range(orbs)])
 
     for o in range(2):
-        both(o, n_band - 1, 6, (bs, br))
+        seven = a0.at[o, pl.ds(0, 14), :, pl.ds(0, NXL)]
+        nine = g.at[o, pl.ds(0, 3), pl.ds(0, 6)]
+        pltpu.make_async_copy(seven, seven, br.at[o]).wait()
+        pltpu.make_async_copy(nine, nine, bs.at[o]).wait()
     for index, dst in enumerate((r1, r2, r3)):
         pltpu.make_async_copy(dst, dst, rs.at[index]).wait()
 
@@ -353,7 +388,7 @@
                 pltpu.VMEM((n_band - 1, 8, 128), F32), pltpu.VMEM((n_gy - 1, 8, 128), F32),
                 pltpu.VMEM((n_gx - 1, 8, 128), F32),
                 sem((2, 2, 8)), sem((2, 2, 8)), sem((4,)), sem((4,)),
-                sem((2,)), sem((2,)), sem((2,)), sem((2,)), sem((3,)), sem((3,)),
+                sem((2,)), sem((2,)), sem((2,)), sem((2,)), sem((2,)), sem((3,)), sem((3,)),
             ],
             compiler_params=pltpu.CompilerParams(
                 collective_id=0, has_side_effects=True, vmem_limit_bytes=32 * 1024 * 1024),

time: 72.2 us -> 70 us (0.970)
  the two profiles are of different devices: /device:TPU:24 before, /device:TPU:4 now
where the time goes in v3:
time: 70 us; the launch traced here: 69.8 us
  Pallas kernels  66.3 us (95%)
  local copies, waits for them, and re-layouts  3.44 us (5%)
    pallas_call x1, Pallas kernels, per_device(): pl.pallas_call(functools.partial(kernel, sizes), out_shape=jax.ShapeDtype...  66.3 us
    unnamed x7, local copies, waits for them, and re-layouts  3.44 us

profile of v3, /device:TPU:4, one launch (start us, length us, event | category | flops | bytes accessed | tf_op | source)
XLA Modules:
  0.0 69.8 jit_solution(1218813334635899289)
XLA Ops:
  0.0 0.0 copy-start
  0.0 1.0 %copy-done = f32[2,32,8,256]{3,2,1,0:T(8,128)S(1)} copy-done((f32[2,32,8,256]{3,2,1,0:T(8,128)S(1)}, f32[2,32,8,256]{3,2,1,0:T(8,128)}, u32[]{:S(2)}) %copy-start) | copy-done | bytes 524312
  1.0 0.0 copy-start.1
  1.0 0.9 %copy-done.1 = f32[32,8,256]{2,1,0:T(8,128)S(1)} copy-done((f32[32,8,256]{2,1,0:T(8,128)S(1)}, f32[32,8,256]{2,1,0:T(8,128)}, u32[]{:S(2)}) %copy-start.1) | copy-done | bytes 262168
  2.0 0.0 copy-start.2
  2.0 0.7 copy-done.2
  2.6 66.3 %shard_map.37 = f32[2,32,8,256]{3,2,1,0:T(8,128)S(1)} custom-call(f32[2,32,8,256]{3,2,1,0:T(8,128)S(1)} %copy-done, f32[32,8,256]{2,1,0:T(8,128)S(1)} %copy-done.1, s32[8]{0:T(128)S(1)} %copy-done.2), custom_call_target="tpu_custom_call" | custom-call | tf_op jit(solution)/shard_map/pallas_call | solution.py:375
  69.0 0.8 %copy.5 = f32[2,32,8,256]{3,2,1,0:T(8,128)} copy(f32[2,32,8,256]{3,2,1,0:T(8,128)S(1)} %shard_map.37) | data formatting | bytes 1048576
Async XLA Ops:
  0.0 1.0 %copy-start = (f32[2,32,8,256]{3,2,1,0:T(8,128)S(1)}, f32[2,32,8,256]{3,2,1,0:T(8,128)}, u32[]{:S(2)}) copy-start(f32[2,32,8,256]{3,2,1,0:T(8,128)} %orb_ref.1) | copy-start | bytes 1572868
  1.0 0.9 %copy-start.1 = (f32[32,8,256]{2,1,0:T(8,128)S(1)}, f32[32,8,256]{2,1,0:T(8,128)}, u32[]{:S(2)}) copy-start(f32[32,8,256]{2,1,0:T(8,128)} %pot_ref.1) | copy-start | bytes 786436
  2.0 0.7 copy-start.2
